TPU v7x, 32 devices: a whole 2x2x4 slice. The times are simulated.
32 devices in a mesh: dp: 4 (over y, x), concept: 8 (over z, core).
Axes of the slice: x: 2, y: 2, z: 4, core: 2. Of those that a mesh axis runs over, the one named last changes fastest.
Arguments:
- embeddings: bfloat16 [32768, 1024], P(('dp', 'concept')), may hold values from -720 to 720
- row_weight: bfloat16 [32768], P(('dp', 'concept')), may hold values from 0.25 to 4
- group_label: int32 [32768, 1], P(('dp', 'concept')), may hold values from 0 to 7; in each aligned block of 1024 rows (0 to 1023, 1024 to 2047, ...) at most 256 rows name the same one
- concept_label: int32 [32768], P(('dp', 'concept')), may hold values from 0 to 1023
- level1_weight: bfloat16 [1024, 8], replicated, may hold values from -0.1875 to 0.1875
- level2_weight: bfloat16 [8, 1024, 1024], P('concept'), may hold values from -0.1875 to 0.1875
Outputs:
- row_loss: float32 [32768], P(('dp', 'concept'))
- embed_grad: bfloat16 [32768, 1024], P(('dp', 'concept'))
- level1_grad: float32 [1024, 8], replicated
- level2_grad: bfloat16 [8, 1024, 1024], P('concept', 'dp')
Inputs may be any that keep to these rules, and one draw needn't show every extreme that they name: `group_label`: among the rows of one device, no group is named more than 256 times, a bound that some block reaches.
All inputs are finite; a program needn't handle non-finite values.
Results may differ from a plain program's by a relative error of at most 0.0051.
Values may be sent and summed in bfloat16 or wider, within the bound.
No kernel may reach another device: no remote copies, remote signals or barrier semaphores. Data moves between devices by JAX's collectives and lax.ppermute only.
A program may use at most 128 MiB of HBM per device.

v0:
```python
import jax
import jax.numpy as jnp
from jax import lax
from jax.sharding import PartitionSpec as P


def first_level(embeddings, weights, groups, level1_weight):
    groups_n = level1_weight.shape[1]
    z1 = jnp.dot(embeddings, level1_weight, preferred_element_type=jnp.float32)
    top1 = jnp.max(z1, axis=1, keepdims=True)
    exps1 = jnp.exp(z1 - top1)
    total1 = jnp.sum(exps1, axis=1, keepdims=True)
    probs1 = exps1 / total1
    onehot1 = (groups[:, None] == jnp.arange(groups_n, dtype=jnp.int32)[None, :]).astype(
        jnp.float32
    )
    loss1 = top1[:, 0] + jnp.log(total1[:, 0]) - jnp.sum(z1 * onehot1, axis=1)
    dz1 = (weights[:, None] * (probs1 - onehot1)).astype(jnp.bfloat16)
    partial_grad = lax.dot_general(
        embeddings, dz1, (((0,), (0,)), ((), ())), preferred_element_type=jnp.float32
    )
    dx1 = jnp.dot(dz1, level1_weight.T, preferred_element_type=jnp.float32)
    level1_grad = lax.psum(partial_grad, ("dp", "concept"))
    return (loss1, dx1, level1_grad)


def on_device(embeddings, row_weight, group_label, concept_label, level1_weight, level2_weight):
    rows_n, width = embeddings.shape
    groups_n = level1_weight.shape[1]
    concepts = level2_weight.shape[2]
    capacity = 2 * rows_n // groups_n
    groups = group_label[:, 0]
    weights = row_weight.astype(jnp.float32)
    member = (groups[:, None] == jnp.arange(groups_n, dtype=jnp.int32)[None, :]).astype(
        jnp.bfloat16
    )
    positions = jnp.arange(rows_n, dtype=jnp.int32)
    earlier = (positions[None, :] < positions[:, None]).astype(jnp.bfloat16)
    before = jnp.dot(earlier, member, preferred_element_type=jnp.float32)
    rank = jnp.sum(before * member.astype(jnp.float32), axis=1).astype(jnp.int32)
    slot = groups * capacity + rank
    source = jnp.full((groups_n * capacity,), rows_n, jnp.int32).at[slot].set(positions)
    filled = source < rows_n
    safe = jnp.minimum(source, rows_n - 1)
    send_rows = jnp.where(filled[:, None], embeddings[safe], jnp.zeros((), jnp.bfloat16)).reshape(
        groups_n, capacity, width
    )
    send_weight = jnp.where(filled, row_weight[safe], jnp.zeros((), jnp.bfloat16)).reshape(
        groups_n, capacity
    )
    send_label = jnp.where(filled, concept_label[safe], 0).reshape(groups_n, capacity)
    loss1, dx1, level1_grad = first_level(embeddings, weights, groups, level1_weight)
    recv_rows, recv_weight, recv_label = (
        lax.all_to_all(send_rows, "concept", split_axis=0, concat_axis=1, tiled=True),
        lax.all_to_all(send_weight, "concept", split_axis=0, concat_axis=1, tiled=True),
        lax.all_to_all(send_label, "concept", split_axis=0, concat_axis=1, tiled=True),
    )
    z2 = jnp.einsum("grd,gdc->grc", recv_rows, level2_weight, preferred_element_type=jnp.float32)
    top2 = jnp.max(z2, axis=2, keepdims=True)
    exps2 = jnp.exp(z2 - top2)
    total2 = jnp.sum(exps2, axis=2, keepdims=True)
    probs2 = exps2 / total2
    onehot2 = (
        recv_label[:, :, None] == jnp.arange(concepts, dtype=jnp.int32)[None, None, :]
    ).astype(jnp.float32)
    loss2 = (top2[:, :, 0] + jnp.log(total2[:, :, 0]) - jnp.sum(z2 * onehot2, axis=2)).astype(
        jnp.bfloat16
    )
    dz2 = (recv_weight.astype(jnp.float32)[:, :, None] * (probs2 - onehot2)).astype(jnp.bfloat16)
    dx2 = jnp.einsum("grc,gdc->grd", dz2, level2_weight, preferred_element_type=jnp.float32).astype(
        jnp.bfloat16
    )
    back_grad, back_loss = (
        lax.all_to_all(dx2, "concept", split_axis=1, concat_axis=0, tiled=True),
        lax.all_to_all(loss2, "concept", split_axis=1, concat_axis=0, tiled=True),
    )
    summed = lax.psum_scatter(
        jnp.einsum("grd,grc->dgc", recv_rows, dz2, preferred_element_type=jnp.float32),
        "dp",
        scatter_dimension=0,
        tiled=True,
    )
    level2_grad = jnp.transpose(summed, (1, 0, 2)).astype(jnp.bfloat16)
    dx2_rows = back_grad.reshape(groups_n * capacity, width)[slot]
    loss2_rows = back_loss.reshape(groups_n * capacity)[slot]
    embed_grad = (dx1 + dx2_rows.astype(jnp.float32)).astype(jnp.bfloat16)
    row_loss = loss1 + loss2_rows.astype(jnp.float32)
    return (row_loss, embed_grad, level1_grad, level2_grad)


def solution(mesh):
    return jax.shard_map(
        on_device,
        mesh=mesh,
        in_specs=(
            P(("dp", "concept"), None),
            P(("dp", "concept")),
            P(("dp", "concept"), None),
            P(("dp", "concept")),
            P(),
            P("concept", None, None),
        ),
        out_specs=(P(("dp", "concept")), P(("dp", "concept"), None), P(), P("concept", "dp", None)),
        check_vma=False,
    )
```

profile of v0, /device:TPU:0, one launch (start us, length us, event | category | flops | bytes accessed | tf_op | source)
XLA Modules:
  0.0 421.7 jit_solution(6824636984605057728)
XLA Ops:
  9.2 4.3 %scatter_custom_fusion = s32[2048]{0:T(1024)S(1)} fusion(s32[1024]{0:T(1024)S(1)} %bitcast.59, s32[1024]{0:T(1024)S(1)} %iota.19, s32[]{:T(128)} %constant.2.clone.1), kind=kCustom, calls=%fused_computation.39 | custom fusion | bytes 8196 | tf_op jit(solution)/shard_map/scatter | solution.py:42
  13.6 11.5 %gather_fusion.3 = bf16[2048]{0:T(1024)(128)(2,1)S(1)} fusion(bf16[1024]{0:T(1024)(128)(2,1)} %param.7, s32[2048]{0:T(1024)S(1)} %fusion.10), kind=kCustom, calls=%fused_computation.3 | custom fusion | bytes 16384 | tf_op jit(solution)/shard_map/gather | solution.py:48
  26.9 6.4 %all-to-all-start.3 = ((bf16[8,2,128]{2,1,0:T(2,128)(2,1)}), bf16[8,2,128]{2,1,0:T(2,128)(2,1)S(1)}, u32[]{:S(2)}, u32[]{:S(2)}) async-start(bf16[8,2,128]{2,1,0:T(2,128)(2,1)} %reshape.239), calls=%async_computation.3 | async-start | bytes 8192 | tf_op jit(solution)/shard_map/all_to_all | solution.py:55
  33.2 12.8 %gather_fusion = bf16[2048,1024]{1,0:T(8,128)(2,1)} fusion(bf16[1024,1024]{1,0:T(8,128)(2,1)} %param.6, s32[2048]{0:T(1024)S(1)} %fusion.10), kind=kCustom, calls=%fused_computation | custom fusion | bytes 8396800 | tf_op jit(solution)/shard_map/gather | solution.py:45
  46.1 3.8 broadcast_select_fusion
  49.9 5.2 %all-to-all-start = ((bf16[8,256,1024]{2,1,0:T(8,128)(2,1)}), bf16[8,256,1024]{2,1,0:T(8,128)(2,1)}, u32[]{:S(2)}, u32[]{:S(2)}) async-start(bf16[8,256,1024]{2,1,0:T(8,128)(2,1)} %broadcast_select_fusion), calls=%async_computation | async-start | bytes 8388608 | tf_op jit(solution)/shard_map/all_to_all | solution.py:54
  55.1 8.6 %gather_fusion.1 = s32[2048]{0:T(1024)S(1)} fusion(s32[1024]{0:T(1024)S(1)} %copy-done.2, s32[2048]{0:T(1024)S(1)} %fusion.10), kind=kCustom, calls=%fused_computation.1 | custom fusion | bytes 24576 | tf_op jit(solution)/shard_map/gather | solution.py:51
  64.3 84.9 %all-to-all-done = bf16[8,256,1024]{2,1,0:T(8,128)(2,1)} async-done(((bf16[8,256,1024]{2,1,0:T(8,128)(2,1)}), bf16[8,256,1024]{2,1,0:T(8,128)(2,1)}, u32[]{:S(2)}, u32[]{:S(2)}) %all-to-all-start) | async-done | bytes 4194336 | tf_op jit(solution)/shard_map/all_to_all | solution.py:54
  149.2 3.3 all-to-all-start.1
  152.6 9.0 %fusion.13 = (f32[2048]{0:T(1024)S(1)}, f32[2048,1024]{0,1:T(8,128)}) fusion(bf16[2048,1024]{1,0:T(8,128)(2,1)} %bitcast.4, bf16[1,1024,1024]{2,1,0:T(8,128)(2,1)S(1)} %copy-done), kind=kOutput, calls=%fused_computation.43 | convolution fusion | flops 4297062400 | bytes 14688256 | tf_op jit(solution)/shard_map/grd,gdc->grc/dot_general | solution.py:58
  161.6 4.7 %fusion = (f32[2048]{0:T(1024)S(1)}, f32[2048]{0:T(1024)S(1)}) fusion(f32[2048,1024]{0,1:T(8,128)} %get-tuple-element.27, f32[2048]{0:T(1024)S(1)} %get-tuple-element.26, s32[2048]{0:T(1024)S(1)} %bitcast.51), kind=kLoop, calls=%fused_computation.10 | loop fusion | flops 10481664 | bytes 8421376 | tf_op jit(solution)/shard_map/reduce_sum | solution.py:61
  172.0 8.2 %convolution_bitcast_fusion = f32[1024,1,1024]{0,2,1:T(8,128)} fusion(bf16[2048,1024]{0,1:T(8,128)(2,1)S(1)} %multiply_convert_fusion, bf16[2048,1024]{1,0:T(8,128)(2,1)} %bitcast.4), kind=kOutput, calls=%fused_computation.17 | convolution fusion | flops 4294967296 | bytes 12582912 | tf_op jit(solution)/shard_map/grd,grc->dgc/dot_general | solution.py:78
  181.4 5.0 %all-to-all-start.2 = ((bf16[8,2,128]{2,1,0:T(2,128)(2,1)}), bf16[8,2,128]{2,1,0:T(2,128)(2,1)S(1)}, u32[]{:S(2)}, u32[]{:S(2)}) async-start(bf16[8,2,128]{2,1,0:T(2,128)(2,1)} %reshape.237), calls=%async_computation.2 | async-start | bytes 8192 | tf_op jit(solution)/shard_map/all_to_all | solution.py:75
  186.4 7.5 %convert_bitcast_fusion = bf16[1,2048,1024]{2,1,0:T(8,128)(2,1)S(1)} fusion(bf16[2048,1024]{0,1:T(8,128)(2,1)} %copy-done.5, bf16[1,1024,1024]{2,1,0:T(8,128)(2,1)S(1)} %copy-done), kind=kOutput, calls=%fused_computation.13 | convolution fusion | flops 4297064448 | bytes 10485760 | tf_op jit(solution)/shard_map/grc,gdc->grd/dot_general | solution.py:70
  193.9 28.7 %copy.24 = bf16[1,2048,1024]{2,0,1:T(2,128)(2,1)} copy(bf16[1,2048,1024]{2,1,0:T(8,128)(2,1)S(1)} %convert_bitcast_fusion) | data formatting | bytes 8388608 | tf_op jit(solution)/shard_map/convert_element_type | solution.py:70
  222.6 26.0 %reduce.10 = bf16[2048,1024]{1,0:T(8,128)(2,1)} reduce(bf16[2048,1,1024]{2,1,0:T(2,128)(2,1)} %bitcast.48, bf16[]{:T(256)} %broadcast.72), dimensions={1}, to_apply=%bitcast.44.reduce_sub_computation | reduce | bytes 8388610
  248.6 7.8 %reshape.241 = bf16[8,2,131072]{2,1,0:T(2,128)(2,1)} reshape(bf16[2048,1024]{1,0:T(8,128)(2,1)} %reduce.10) | data formatting | bytes 8388608
  256.4 5.3 %all-to-all-start.4 = ((bf16[8,2,131072]{2,1,0:T(2,128)(2,1)}), bf16[8,2,131072]{2,1,0:T(2,128)(2,1)}, u32[]{:S(2)}, u32[]{:S(2)}) async-start(bf16[8,2,131072]{2,1,0:T(2,128)(2,1)} %reshape.241), calls=%async_computation.4 | async-start | bytes 8388608 | tf_op jit(solution)/shard_map/all_to_all | solution.py:74
  266.1 110.7 %psum.7 = f32[1024,8]{0,1:T(8,128)} all-reduce(f32[1024,8]{0,1:T(8,128)S(1)} %convolution_bitcast_fusion.1), channel_id=1, replica_groups=mesh['dp'=4,'concept'=8] {'dp','concept'}, use_global_device_ids=true, to_apply=%region_8.9 | all-reduce | flops 8192 | bytes 65536 | tf_op jit(solution)/shard_map/psum | solution.py:23
  376.8 6.8 %gather_fusion.2 = bf16[1024]{0:T(1024)(128)(2,1)S(1)} fusion(bf16[2048]{0:T(1024)(128)(2,1)S(1)} %bitcast.46, s32[1024]{0:T(1024)S(1)} %broadcast_clamp_fusion), kind=kCustom, calls=%fused_computation.2 | custom fusion | bytes 8192 | tf_op jit(solution)/shard_map/gather | solution.py:85
  384.2 8.8 %reshape.242 = bf16[2048,1,1024]{2,1,0:T(2,128)(2,1)} reshape(bf16[8,2,131072]{2,1,0:T(2,128)(2,1)} %all-to-all-done.4) | data formatting | bytes 8388608
  393.0 7.0 %copy.23 = bf16[1,2048,1024]{2,1,0:T(8,128)(2,1)} copy(bf16[1,2048,1024]{2,0,1:T(2,128)(2,1)} %bitcast.49) | data formatting | bytes 8388608
  400.0 8.9 %gather_fusion.4 = bf16[1024,1024]{1,0:T(8,128)(2,1)} fusion(bf16[2048,1024]{1,0:T(8,128)(2,1)} %bitcast.47, s32[1024]{0:T(1024)S(1)} %broadcast_clamp_fusion), kind=kCustom, calls=%fused_computation.4 | custom fusion | bytes 4198400 | tf_op jit(solution)/shard_map/gather | solution.py:84
  408.9 3.7 add_convert_fusion
  (53 shorter events, 18.7 us)
Async XLA Ops:
  7.2 145.4 %copy-start = (bf16[1,1024,1024]{2,1,0:T(8,128)(2,1)S(1)}, bf16[1,1024,1024]{2,1,0:T(8,128)(2,1)}, u32[]{:S(2)}) copy-start(bf16[1,1024,1024]{2,1,0:T(8,128)(2,1)} %param.11) | copy-start | bytes 6291460
  26.9 23.0 %all-to-all-start.3 = ((bf16[8,2,128]{2,1,0:T(2,128)(2,1)}), bf16[8,2,128]{2,1,0:T(2,128)(2,1)S(1)}, u32[]{:S(2)}, u32[]{:S(2)}) async-start(bf16[8,2,128]{2,1,0:T(2,128)(2,1)} %reshape.239), calls=%async_computation.3 | async-start | bytes 8192 | tf_op jit(solution)/shard_map/all_to_all | solution.py:55
  49.9 5.2 %copy-start.2 = (s32[1024]{0:T(1024)S(1)}, s32[1024]{0:T(1024)}, u32[]{:S(2)}) copy-start(s32[1024]{0:T(1024)} %param.9) | copy-start | bytes 12292
  49.9 99.3 %all-to-all-start = ((bf16[8,256,1024]{2,1,0:T(8,128)(2,1)}), bf16[8,256,1024]{2,1,0:T(8,128)(2,1)}, u32[]{:S(2)}, u32[]{:S(2)}) async-start(bf16[8,256,1024]{2,1,0:T(8,128)(2,1)} %broadcast_select_fusion), calls=%async_computation | async-start | bytes 8388608 | tf_op jit(solution)/shard_map/all_to_all | solution.py:54
  149.2 12.4 %all-to-all-start.1 = ((s32[8,1,256]{2,1,0:T(1,128)}), s32[8,1,256]{2,1,0:T(1,128)S(1)}, u32[]{:S(2)}, u32[]{:S(2)}) async-start(s32[8,1,256]{2,1,0:T(1,128)} %bitcast.6), calls=%async_computation.1 | async-start | bytes 16384 | tf_op jit(solution)/shard_map/all_to_all | solution.py:56
  152.5 260.0 %reduce-scatter.2.cloned.1.call-start = ((), (), s32[]{:S(2)}) async-start(), calls=%async_computation.6 | async-start | bytes 5242880 | tf_op jit(solution)/shard_map/reduce_scatter | solution.py:77
  161.6 5.8 %copy-start.4 = (f32[2048,1024]{0,1:T(8,128)S(1)}, f32[2048,1024]{0,1:T(8,128)}, u32[]{:S(2)}) copy-start(f32[2048,1024]{0,1:T(8,128)} %get-tuple-element.27) | copy-start | bytes 25165828
  170.0 1.9 copy-start.5
  181.4 75.0 %all-to-all-start.2 = ((bf16[8,2,128]{2,1,0:T(2,128)(2,1)}), bf16[8,2,128]{2,1,0:T(2,128)(2,1)S(1)}, u32[]{:S(2)}, u32[]{:S(2)}) async-start(bf16[8,2,128]{2,1,0:T(2,128)(2,1)} %reshape.237), calls=%async_computation.2 | async-start | bytes 8192 | tf_op jit(solution)/shard_map/all_to_all | solution.py:75
  256.4 5.3 %copy-start.3 = (bf16[1024]{0:T(1024)(128)(2,1)S(1)}, bf16[1024]{0:T(1024)(128)(2,1)}, u32[]{:S(2)}) copy-start(bf16[1024]{0:T(1024)(128)(2,1)} %param.7) | copy-start | bytes 6148
  256.4 5.4 %copy-start.6 = (bf16[1024,8]{0,1:T(8,128)(2,1)S(1)}, bf16[1024,8]{0,1:T(8,128)(2,1)}, u32[]{:S(2)}) copy-start(bf16[1024,8]{0,1:T(8,128)(2,1)} %param.10) | copy-start | bytes 49156
  256.4 7.6 %copy-start.7 = (s32[1024,1]{0,1:T(1,128)S(1)}, s32[1024,1]{0,1:T(1,128)}, u32[]{:S(2)}) copy-start(s32[1024,1]{0,1:T(1,128)} %param.8) | copy-start | bytes 12292
  256.4 127.8 %all-to-all-start.4 = ((bf16[8,2,131072]{2,1,0:T(2,128)(2,1)}), bf16[8,2,131072]{2,1,0:T(2,128)(2,1)}, u32[]{:S(2)}, u32[]{:S(2)}) async-start(bf16[8,2,131072]{2,1,0:T(2,128)(2,1)} %reshape.241), calls=%async_computation.4 | async-start | bytes 8388608 | tf_op jit(solution)/shard_map/all_to_all | solution.py:74
  400.0 14.8 %copy-start.1 = (bf16[1,1024,1024]{2,1,0:T(8,128)(2,1)S(1)}, bf16[1,1024,1024]{2,1,0:T(8,128)(2,1)}, u32[]{:S(2)}) copy-start(bf16[1,1024,1024]{2,1,0:T(8,128)(2,1)} %param.11) | copy-start | bytes 6291460
Sparse Core Ops, SparseCore 0:
  180.3 53.9 reduce-scatter.1
where the time goes:
time: 423 us; the launch traced here: 422 us
  local copies, waits for them, and re-layouts  111 us (26%)
  blocking collectives  111 us (26%)
  waiting for transfers between devices  84.9 us (20%)
  other arithmetic  41.7 us (10%)
  matrix products  33.9 us (8%)
  starting transfers between devices  25.3 us (6%)
  between operations  14.2 us (3%)
    psum x1, blocking collectives, first_level(): level1_grad = lax.psum(partial_grad, ('dp', 'concept'))  111 us
    all_to_all x1, waiting for transfers between devices, on_device(): lax.all_to_all(send_rows, 'concept', split_axis=0, concat_axis=1, tiled=T...  84.9 us
    unnamed x26, local copies, waits for them, and re-layouts  29.4 us
    convert_element_type x1, local copies, waits for them, and re-layouts, on_device(): jnp.einsum('grc,gdc->grd', dz2, level2_weight, preferred_element_type=jnp...  28.7 us
    unnamed x2, other arithmetic  26.6 us
    gather x1, local copies, waits for them, and re-layouts, on_device(): embeddings[safe]  12.8 us
    gather x1, local copies, waits for them, and re-layouts, on_device(): row_weight[safe]  11.5 us
    dot_general x1, matrix products, on_device(): jnp.einsum('grd,gdc->grc', recv_rows, level2_weight, preferred_element_ty...  9.01 us
  transfers between devices with their start and end apart: 6, of which 1 were waited for; matrix products, arithmetic and copies ran while one was open for 35% of the time, Pallas kernels for 0%

commit v1 on v0

--- a/solution.py
+++ b/solution.py
@@ -20,7 +20,7 @@
         embeddings, dz1, (((0,), (0,)), ((), ())), preferred_element_type=jnp.float32
     )
     dx1 = jnp.dot(dz1, level1_weight.T, preferred_element_type=jnp.float32)
-    level1_grad = lax.psum(partial_grad, ("dp", "concept"))
+    level1_grad = jnp.sum(lax.all_gather(partial_grad, ("dp", "concept")), axis=0)
     return (loss1, dx1, level1_grad)
 
 

time: 423 us -> 401 us (0.948)
  blocking collectives: 111 us -> 0 us
  waiting for transfers between devices: 84.9 us -> 170 us
    psum x1 -> x0, blocking collectives: 111 us -> none  [first_level(): level1_grad = lax.psum(partial_grad, ('dp', 'concept'))]
    all_to_all x1, waiting for transfers between devices: 0.01 us -> 84.7 us  [on_device(): lax.all_to_all(dx2, 'concept', split_axis=1, concat_axis=0, tiled=True)]
    unnamed x26 -> x24, local copies, waits for them, and re-layouts: 29.4 us -> 28.3 us
  transfers between devices with their start and end apart: 6 -> 7, of which waited for: 1 -> 2; matrix products, arithmetic and copies ran while one was open for 35% -> 41% of each run, Pallas kernels for 0% -> 0%
where the time goes in v1:
time: 401 us; the launch traced here: 400 us
  waiting for transfers between devices  170 us (42%)
  local copies, waits for them, and re-layouts  110 us (27%)
  other arithmetic  45.7 us (11%)
  matrix products  34.1 us (9%)
  starting transfers between devices  25.1 us (6%)
  between operations  15.7 us (4%)
    all_to_all x1, waiting for transfers between devices, on_device(): lax.all_to_all(send_rows, 'concept', split_axis=0, concat_axis=1, tiled=T...  84.8 us
    all_to_all x1, waiting for transfers between devices, on_device(): lax.all_to_all(dx2, 'concept', split_axis=1, concat_axis=0, tiled=True)  84.7 us
    convert_element_type x1, local copies, waits for them, and re-layouts, on_device(): jnp.einsum('grc,gdc->grd', dz2, level2_weight, preferred_element_type=jnp...  28.7 us
    unnamed x24, local copies, waits for them, and re-layouts  28.3 us
    unnamed x2, other arithmetic  26.6 us
    gather x1, local copies, waits for them, and re-layouts, on_device(): embeddings[safe]  12.8 us
    gather x1, local copies, waits for them, and re-layouts, on_device(): row_weight[safe]  11.5 us
    dot_general x1, matrix products, on_device(): jnp.einsum('grd,gdc->grc', recv_rows, level2_weight, preferred_element_ty...  9.01 us
  transfers between devices with their start and end apart: 7, of which 2 were waited for; matrix products, arithmetic and copies ran while one was open for 41% of the time, Pallas kernels for 0%

profile of v1, /device:TPU:0, one launch (start us, length us, event | category | flops | bytes accessed | tf_op | source)
XLA Modules:
  0.0 400.1 jit_solution(4026492664921054478)
XLA Ops:
  10.1 4.3 %scatter_custom_fusion = s32[2048]{0:T(1024)S(1)} fusion(s32[1024]{0:T(1024)S(1)} %bitcast.61, s32[1024]{0:T(1024)S(1)} %iota.19, s32[]{:T(128)} %constant.2.clone.1), kind=kCustom, calls=%fused_computation.39 | custom fusion | bytes 8196 | tf_op jit(solution)/shard_map/scatter | solution.py:42
  14.4 11.5 %gather_fusion.3 = bf16[2048]{0:T(1024)(128)(2,1)S(1)} fusion(bf16[1024]{0:T(1024)(128)(2,1)} %param.7, s32[2048]{0:T(1024)S(1)} %fusion.10), kind=kCustom, calls=%fused_computation.3 | custom fusion | bytes 16384 | tf_op jit(solution)/shard_map/gather | solution.py:48
  27.7 6.4 %all-to-all-start.3 = ((bf16[8,2,128]{2,1,0:T(2,128)(2,1)}), bf16[8,2,128]{2,1,0:T(2,128)(2,1)S(1)}, u32[]{:S(2)}, u32[]{:S(2)}) async-start(bf16[8,2,128]{2,1,0:T(2,128)(2,1)} %reshape.240), calls=%async_computation.3 | async-start | bytes 8192 | tf_op jit(solution)/shard_map/all_to_all | solution.py:55
  34.1 12.8 %gather_fusion = bf16[2048,1024]{1,0:T(8,128)(2,1)} fusion(bf16[1024,1024]{1,0:T(8,128)(2,1)} %param.6, s32[2048]{0:T(1024)S(1)} %fusion.10), kind=kCustom, calls=%fused_computation | custom fusion | bytes 8396800 | tf_op jit(solution)/shard_map/gather | solution.py:45
  46.9 3.8 broadcast_select_fusion
  50.7 5.2 %all-to-all-start = ((bf16[8,256,1024]{2,1,0:T(8,128)(2,1)}), bf16[8,256,1024]{2,1,0:T(8,128)(2,1)}, u32[]{:S(2)}, u32[]{:S(2)}) async-start(bf16[8,256,1024]{2,1,0:T(8,128)(2,1)} %broadcast_select_fusion), calls=%async_computation | async-start | bytes 8388608 | tf_op jit(solution)/shard_map/all_to_all | solution.py:54
  61.0 8.6 %gather_fusion.1 = s32[2048]{0:T(1024)S(1)} fusion(s32[1024]{0:T(1024)S(1)} %copy-done.2, s32[2048]{0:T(1024)S(1)} %fusion.10), kind=kCustom, calls=%fused_computation.1 | custom fusion | bytes 24576 | tf_op jit(solution)/shard_map/gather | solution.py:51
  70.2 84.8 %all-to-all-done = bf16[8,256,1024]{2,1,0:T(8,128)(2,1)} async-done(((bf16[8,256,1024]{2,1,0:T(8,128)(2,1)}), bf16[8,256,1024]{2,1,0:T(8,128)(2,1)}, u32[]{:S(2)}, u32[]{:S(2)}) %all-to-all-start) | async-done | bytes 4194336 | tf_op jit(solution)/shard_map/all_to_all | solution.py:54
  158.4 9.0 %fusion.13 = (f32[2048]{0:T(1024)S(1)}, f32[2048,1024]{0,1:T(8,128)}) fusion(bf16[2048,1024]{1,0:T(8,128)(2,1)} %bitcast.4, bf16[1,1024,1024]{2,1,0:T(8,128)(2,1)S(1)} %copy-done), kind=kOutput, calls=%fused_computation.43 | convolution fusion | flops 4297062400 | bytes 14688256 | tf_op jit(solution)/shard_map/grd,gdc->grc/dot_general | solution.py:58
  167.4 4.6 %fusion = (f32[2048]{0:T(1024)S(1)}, f32[2048]{0:T(1024)S(1)}) fusion(f32[2048,1024]{0,1:T(8,128)} %get-tuple-element.27, f32[2048]{0:T(1024)S(1)} %get-tuple-element.26, s32[2048]{0:T(1024)S(1)} %bitcast.53), kind=kLoop, calls=%fused_computation.10 | loop fusion | flops 10481664 | bytes 8421376 | tf_op jit(solution)/shard_map/reduce_sum | solution.py:61
  173.3 5.0 %all-to-all-start.2 = ((bf16[8,2,128]{2,1,0:T(2,128)(2,1)}), bf16[8,2,128]{2,1,0:T(2,128)(2,1)S(1)}, u32[]{:S(2)}, u32[]{:S(2)}) async-start(bf16[8,2,128]{2,1,0:T(2,128)(2,1)} %reshape.238), calls=%async_computation.2 | async-start | bytes 8192 | tf_op jit(solution)/shard_map/all_to_all | solution.py:75
  178.6 4.8 %multiply_convert_fusion = bf16[2048,1024]{0,1:T(8,128)(2,1)S(1)} fusion(f32[2048,1024]{0,1:T(8,128)} %get-tuple-element.27, f32[2048]{0:T(1024)S(1)} %get-tuple-element.20, f32[2048]{0:T(1024)S(1)} %bitcast.59, s32[2048]{0:T(1024)S(1)} %bitcast.54, f32[2048]{0:T(1024)S(1)} %get-tuple-element.26), kind=kLoop, calls=%fused_computation.6 | loop fusion | flops 14680064 | bytes 12615680 | tf_op jit(solution)/shard_map/convert_element_type | solution.py:69
  185.3 8.2 %convolution_bitcast_fusion = f32[1024,1,1024]{0,2,1:T(8,128)} fusion(bf16[2048,1024]{0,1:T(8,128)(2,1)S(1)} %multiply_convert_fusion, bf16[2048,1024]{1,0:T(8,128)(2,1)} %bitcast.4), kind=kOutput, calls=%fused_computation.17 | convolution fusion | flops 4294967296 | bytes 12582912 | tf_op jit(solution)/shard_map/grd,grc->dgc/dot_general | solution.py:78
  193.5 7.0 %convert_bitcast_fusion = bf16[1,2048,1024]{2,1,0:T(8,128)(2,1)S(1)} fusion(bf16[2048,1024]{0,1:T(8,128)(2,1)} %copy-done.4, bf16[1,1024,1024]{2,1,0:T(8,128)(2,1)S(1)} %copy-done), kind=kOutput, calls=%fused_computation.13 | convolution fusion | flops 4297064448 | bytes 10485760 | tf_op jit(solution)/shard_map/grc,gdc->grd/dot_general | solution.py:70
  200.5 28.7 %copy.24 = bf16[1,2048,1024]{2,0,1:T(2,128)(2,1)} copy(bf16[1,2048,1024]{2,1,0:T(8,128)(2,1)S(1)} %convert_bitcast_fusion) | data formatting | bytes 8388608 | tf_op jit(solution)/shard_map/convert_element_type | solution.py:70
  229.2 26.0 %reduce.10 = bf16[2048,1024]{1,0:T(8,128)(2,1)} reduce(bf16[2048,1,1024]{2,1,0:T(2,128)(2,1)} %bitcast.49, bf16[]{:T(256)} %broadcast.72), dimensions={1}, to_apply=%bitcast.45.reduce_sub_computation | reduce | bytes 8388610
  255.2 7.8 %reshape.242 = bf16[8,2,131072]{2,1,0:T(2,128)(2,1)} reshape(bf16[2048,1024]{1,0:T(8,128)(2,1)} %reduce.10) | data formatting | bytes 8388608
  263.0 4.9 %all-to-all-start.4 = ((bf16[8,2,131072]{2,1,0:T(2,128)(2,1)}), bf16[8,2,131072]{2,1,0:T(2,128)(2,1)}, u32[]{:S(2)}, u32[]{:S(2)}) async-start(bf16[8,2,131072]{2,1,0:T(2,128)(2,1)} %reshape.242), calls=%async_computation.4 | async-start | bytes 8388608 | tf_op jit(solution)/shard_map/all_to_all | solution.py:74
  269.9 6.8 %gather_fusion.2 = bf16[1024]{0:T(1024)(128)(2,1)S(1)} fusion(bf16[2048]{0:T(1024)(128)(2,1)S(1)} %bitcast.47, s32[1024]{0:T(1024)S(1)} %broadcast_clamp_fusion), kind=kCustom, calls=%fused_computation.2 | custom fusion | bytes 8192 | tf_op jit(solution)/shard_map/gather | solution.py:85
  277.3 84.7 %all-to-all-done.4 = bf16[8,2,131072]{2,1,0:T(2,128)(2,1)} async-done(((bf16[8,2,131072]{2,1,0:T(2,128)(2,1)}), bf16[8,2,131072]{2,1,0:T(2,128)(2,1)}, u32[]{:S(2)}, u32[]{:S(2)}) %all-to-all-start.4) | async-done | bytes 4194336 | tf_op jit(solution)/shard_map/all_to_all | solution.py:74
  362.0 8.8 %reshape.243 = bf16[2048,1,1024]{2,1,0:T(2,128)(2,1)} reshape(bf16[8,2,131072]{2,1,0:T(2,128)(2,1)} %all-to-all-done.4) | data formatting | bytes 8388608
  370.7 7.0 %copy.23 = bf16[1,2048,1024]{2,1,0:T(8,128)(2,1)} copy(bf16[1,2048,1024]{2,0,1:T(2,128)(2,1)} %bitcast.50) | data formatting | bytes 8388608
  377.8 8.9 %gather_fusion.4 = bf16[1024,1024]{1,0:T(8,128)(2,1)} fusion(bf16[2048,1024]{1,0:T(8,128)(2,1)} %bitcast.48, s32[1024]{0:T(1024)S(1)} %broadcast_clamp_fusion), kind=kCustom, calls=%fused_computation.4 | custom fusion | bytes 4198400 | tf_op jit(solution)/shard_map/gather | solution.py:84
  386.6 3.7 add_convert_fusion
  (54 shorter events, 21.1 us)
Async XLA Ops:
  8.0 150.4 %copy-start = (bf16[1,1024,1024]{2,1,0:T(8,128)(2,1)S(1)}, bf16[1,1024,1024]{2,1,0:T(8,128)(2,1)}, u32[]{:S(2)}) copy-start(bf16[1,1024,1024]{2,1,0:T(8,128)(2,1)} %param.11) | copy-start | bytes 6291460
  27.7 23.0 %all-to-all-start.3 = ((bf16[8,2,128]{2,1,0:T(2,128)(2,1)}), bf16[8,2,128]{2,1,0:T(2,128)(2,1)S(1)}, u32[]{:S(2)}, u32[]{:S(2)}) async-start(bf16[8,2,128]{2,1,0:T(2,128)(2,1)} %reshape.240), calls=%async_computation.3 | async-start | bytes 8192 | tf_op jit(solution)/shard_map/all_to_all | solution.py:55
  50.7 5.3 %copy-start.3 = (bf16[1024]{0:T(1024)(128)(2,1)S(1)}, bf16[1024]{0:T(1024)(128)(2,1)}, u32[]{:S(2)}) copy-start(bf16[1024]{0:T(1024)(128)(2,1)} %param.7) | copy-start | bytes 6148
  50.7 5.3 %copy-start.5 = (bf16[1024,8]{0,1:T(8,128)(2,1)S(1)}, bf16[1024,8]{0,1:T(8,128)(2,1)}, u32[]{:S(2)}) copy-start(bf16[1024,8]{0,1:T(8,128)(2,1)} %param.10) | copy-start | bytes 49156
  50.7 7.6 %copy-start.6 = (s32[1024,1]{0,1:T(1,128)S(1)}, s32[1024,1]{0,1:T(1,128)}, u32[]{:S(2)}) copy-start(s32[1024,1]{0,1:T(1,128)} %param.8) | copy-start | bytes 12292
  50.7 104.3 %all-to-all-start = ((bf16[8,256,1024]{2,1,0:T(8,128)(2,1)}), bf16[8,256,1024]{2,1,0:T(8,128)(2,1)}, u32[]{:S(2)}, u32[]{:S(2)}) async-start(bf16[8,256,1024]{2,1,0:T(8,128)(2,1)} %broadcast_select_fusion), calls=%async_computation | async-start | bytes 8388608 | tf_op jit(solution)/shard_map/all_to_all | solution.py:54
  55.9 5.0 %copy-start.2 = (s32[1024]{0:T(1024)S(1)}, s32[1024]{0:T(1024)}, u32[]{:S(2)}) copy-start(s32[1024]{0:T(1024)} %param.9) | copy-start | bytes 12292
  56.0 212.0 %all-gather.3.cloned.1.call-start = ((), (), s32[]{:S(2)}) async-start(), calls=%async_computation.7 | async-start | bytes 1081344 | tf_op jit(solution)/shard_map/all_gather | solution.py:23
  155.0 12.4 %all-to-all-start.1 = ((s32[8,1,256]{2,1,0:T(1,128)}), s32[8,1,256]{2,1,0:T(1,128)S(1)}, u32[]{:S(2)}, u32[]{:S(2)}) async-start(s32[8,1,256]{2,1,0:T(1,128)} %bitcast.6), calls=%async_computation.1 | async-start | bytes 16384 | tf_op jit(solution)/shard_map/all_to_all | solution.py:56
  173.3 89.7 %all-to-all-start.2 = ((bf16[8,2,128]{2,1,0:T(2,128)(2,1)}), bf16[8,2,128]{2,1,0:T(2,128)(2,1)S(1)}, u32[]{:S(2)}, u32[]{:S(2)}) async-start(bf16[8,2,128]{2,1,0:T(2,128)(2,1)} %reshape.238), calls=%async_computation.2 | async-start | bytes 8192 | tf_op jit(solution)/shard_map/all_to_all | solution.py:75
  178.3 212.0 %reduce-scatter.2.cloned.1.call-start = ((), (), s32[]{:S(2)}) async-start(), calls=%async_computation.6 | async-start | bytes 5242880 | tf_op jit(solution)/shard_map/reduce_scatter | solution.py:77
  183.4 1.9 copy-start.4
  263.0 98.9 %all-to-all-start.4 = ((bf16[8,2,131072]{2,1,0:T(2,128)(2,1)}), bf16[8,2,131072]{2,1,0:T(2,128)(2,1)}, u32[]{:S(2)}, u32[]{:S(2)}) async-start(bf16[8,2,131072]{2,1,0:T(2,128)(2,1)} %reshape.242), calls=%async_computation.4 | async-start | bytes 8388608 | tf_op jit(solution)/shard_map/all_to_all | solution.py:74
  377.8 14.8 %copy-start.1 = (bf16[1,1024,1024]{2,1,0:T(8,128)(2,1)S(1)}, bf16[1,1024,1024]{2,1,0:T(8,128)(2,1)}, u32[]{:S(2)}) copy-start(bf16[1,1024,1024]{2,1,0:T(8,128)(2,1)} %param.11) | copy-start | bytes 6291460
Sparse Core Ops, SparseCore 0:
  61.1 75.1 all-gather.2
Sparse Core Ops, SparseCore 1:
  193.6 53.7 reduce-scatter.1
